TPU v7x, 128 devices: a whole 4x4x4 slice. The times are simulated.
128 devices in a mesh: len: 16 (over z, x), xs: 8 (over y, core).
Axes of the slice: x: 4, y: 4, z: 4, core: 2. Of those that a mesh axis runs over, the one named last changes fastest.
Arguments:
- right_side: float32 [3, 16, 64, 16384], P(None, None, None, ('len', 'xs')), may hold values from -19 to 19
- mass_field: float32 [16, 64, 16384], P(None, None, ('len', 'xs')), may hold values from 0.5 to 2
- span_lengths: int32 [128], replicated, may hold values from 1 to 256, 16384 in all
- stick_flags: int32 [256], replicated, may hold values from 0 to 1
- normal_load: float32 [256], replicated, may hold values from 0.5 to 4
- prior_friction: float32 [2, 256], replicated, may hold values from -4 to 4
Outputs:
- increment: float32 [3, 16, 64, 16384], P(None, None, None, ('len', 'xs'))
- residual: float32 [3, 16, 64, 16384], P(None, None, None, ('len', 'xs'))
- friction: float32 [2, 256], replicated
Inputs may be any that keep to these rules, and one draw needn't show every extreme that they name: `span_lengths`: the spans sum to 16384; the longest is exactly 256. `stick_flags`: 1 marks a sticking bearing, 0 a sliding one.
All inputs are finite; a program needn't handle non-finite values.
Results may differ from a plain program's by a relative error of at most 0.0003.
Values sent between devices are 32-bit elements; how exact they have to be, the bound alone decides.
A program may use at most 64 MiB of HBM per device.

v0:
```python
import jax
import jax.numpy as jnp
from jax import lax
from jax.sharding import PartitionSpec as P

ITERS = 3
shear_modulus = 1.0
bulk_modulus = 1.5
elastic_stiffness = 8.0
pendulum_radius = 4.0
vertical_stiffness = 5.0
static_friction = 0.6
kinetic_friction = 0.45


def extended_2(cells, sides, width):
    for axis, dim in sides:
        count = lax.axis_size(axis)
        ends = count - 1
        head = lax.slice_in_dim(cells, 0, width, axis=dim)
        tail = lax.slice_in_dim(cells, cells.shape[dim] - width, cells.shape[dim], axis=dim)
        cells = jnp.concatenate(
            [
                lax.ppermute(tail, axis, [(i, (i + 1) % count) for i in range(ends)]),
                cells,
                lax.ppermute(head, axis, [((i + 1) % count, i) for i in range(ends)]),
            ],
            axis=dim,
        )
    return cells


def window(array, anchor, extent):
    return array[
        ...,
        anchor[0] : anchor[0] + extent[0],
        anchor[1] : anchor[1] + extent[1],
        anchor[2] : anchor[2] + extent[2],
    ]


def shifted(anchor, along_dim, stride):
    moved = list(anchor)
    moved[along_dim] = moved[along_dim] + stride
    return tuple(moved)


def difference(array, anchor, extent, along_dim):
    upper = window(array, shifted(anchor, along_dim, 1), extent)
    lower = window(array, shifted(anchor, along_dim, -1), extent)
    return 0.5 * (upper - lower)


def laplace_at(padded, anchor, extent):
    total = 6.0 * window(padded, anchor, extent)
    for along_dim in range(3):
        for stride in (1, -1):
            total = total - window(padded, shifted(anchor, along_dim, stride), extent)
    return total


def pad_local(array, width):
    widths = [(0, 0)] * array.ndim
    widths[array.ndim - 3] = (width, width)
    widths[array.ndim - 2] = (width, width)
    return jnp.pad(array, widths)


def operate(field, mass_field):
    dims_of = (2, 1, 0)
    extent = field.shape[1:]
    extended = extended_2(field, ((("len", "xs"), 3),), 1)
    extended = pad_local(extended, 1)
    divergence = difference(extended[0], (1, 1, 1), extent, dims_of[0])
    for component in (1, 2):
        divergence = divergence + difference(
            extended[component], (1, 1, 1), extent, dims_of[component]
        )
    div_extended = extended_2(divergence, ((("len", "xs"), 2),), 1)
    div_extended = pad_local(div_extended, 1)
    laplacian = laplace_at(extended, (1, 1, 1), extent)
    gradient = jnp.stack(
        [difference(div_extended, (1, 1, 1), extent, dims_of[c]) for c in range(3)]
    )
    return mass_field[None] * field + shear_modulus * laplacian - bulk_modulus * gradient


def return_map(readout, stick_flags, normal_load, prior_friction):
    coeff = jnp.where(stick_flags == 1, static_friction, kinetic_friction)
    radius = coeff * normal_load
    trial = prior_friction + elastic_stiffness * readout[0:2]
    magnitude = jnp.sqrt(trial[0] * trial[0] + trial[1] * trial[1])
    friction = trial * (radius / jnp.maximum(magnitude, radius))
    horizontal = friction + normal_load / pendulum_radius * readout[0:2]
    vertical = vertical_stiffness * readout[2]
    force = jnp.concatenate([horizontal, vertical[None]], axis=0)
    return (friction, force)


def shards(right_side, mass_field, span_lengths, stick_flags, normal_load, prior_friction):
    local_across = right_side.shape[2]
    local_along = right_side.shape[3]
    bearings = 2 * span_lengths.shape[0]
    ends = jnp.cumsum(span_lengths) - 1
    along_site = jnp.repeat(ends, 2)
    across_site = jnp.tile(
        jnp.array([local_across // 4, 3 * local_across // 4], dtype=jnp.int32),
        span_lengths.shape[0],
    )
    along_start = lax.axis_index(("len", "xs")) * local_along
    along_hit = (
        lax.broadcasted_iota(jnp.int32, (local_along, bearings), 0) + along_start
        == along_site[None, :]
    ).astype(jnp.float32)
    across_hit = (
        lax.broadcasted_iota(jnp.int32, (local_across, bearings), 0) == across_site[None, :]
    ).astype(jnp.float32)
    increment = jnp.zeros_like(right_side)
    solved = right_side
    direction = right_side
    norm_now = lax.psum(jnp.sum(solved * solved), ("len", "xs"))
    for iteration in range(ITERS):
        image = operate(direction, mass_field)
        curvature = lax.psum(jnp.sum(direction * image), ("len", "xs"))
        alpha = norm_now / curvature
        increment = increment + alpha * direction
        solved = solved - alpha * image
        norm_next = lax.psum(jnp.sum(solved * solved), ("len", "xs"))
        direction = solved + norm_next / norm_now * direction
        norm_now = norm_next
    picked = jnp.einsum("csl,lb->csb", increment[:, 0], along_hit, precision=lax.Precision.HIGHEST)
    readout = lax.psum(jnp.sum(picked * across_hit[None], axis=1), ("len", "xs"))
    friction, force = return_map(readout, stick_flags, normal_load, prior_friction)
    spread = force[:, None, :] * across_hit[None]
    placed = jnp.einsum("csb,lb->csl", spread, along_hit, precision=lax.Precision.HIGHEST)
    residual = solved.at[:, 0].add(-placed)
    return (increment, residual, friction)


def solution(mesh):
    in_specs = (
        P(None, None, None, ("len", "xs")),
        P(None, None, ("len", "xs")),
        P(),
        P(),
        P(),
        P(),
    )
    out_specs = (P(None, None, None, ("len", "xs")), P(None, None, None, ("len", "xs")), P())
    return jax.shard_map(shards, mesh=mesh, in_specs=in_specs, out_specs=out_specs, check_vma=False)
```

profile of v0, /device:TPU:1, one launch (start us, length us, event | category | flops | bytes accessed | tf_op | source)
XLA Modules:
  0.0 561.3 jit_solution(11000767857912124190)
XLA Ops:
  0.6 2.6 fusion.70
  3.8 4.6 collective-permute-start
  8.9 1.9 collective-permute-start.1
  11.8 2.2 collective-permute-done.1
  14.0 1.7 copy.71
  15.7 3.8 select_maximum_fusion.4
  19.9 0.8 fusion.46
  21.0 2.0 collective-permute-start.2
  23.0 3.6 collective-permute-start.3
  26.7 3.9 multiply_reduce_fusion.5
  30.6 1.0 collective-permute-done.2
  31.6 1.2 collective-permute-done.3
  33.3 1.0 fusion.41
  34.4 1.3 multiply_reduce_fusion.4
  35.7 76.7 %all-reduce.6 = (f32[]{:T(128)}, f32[]{:T(128)}) all-reduce(f32[]{:T(128)} %get-tuple-element.45, f32[]{:T(128)} %multiply_reduce_fusion.4), channel_id=1, replica_groups=mesh['len'=16,'xs'=8] {'len','xs'}, use_global_device_ids=true, to_apply=%region_1.2 | all-reduce | flops 2 | bytes 16 | tf_op jit(solution)/shard_map/psum | solution.py:121
  113.7 3.6 multiply_reduce_fusion.3
  117.3 64.9 %psum.51 = f32[]{:T(128)} all-reduce(f32[]{:T(128)} %get-tuple-element.30), channel_id=1, replica_groups=mesh['len'=16,'xs'=8] {'len','xs'}, use_global_device_ids=true, to_apply=%region_5.6 | all-reduce | flops 1 | bytes 8 | tf_op jit(solution)/shard_map/psum | solution.py:128
  183.5 1.8 multiply_add_fusion.2
  185.3 2.3 fusion.69
  187.6 1.9 copy.82
  189.5 1.9 collective-permute-start.4
  191.4 1.9 copy.83
  193.3 2.4 collective-permute-start.5
  195.9 1.3 copy.80
  197.2 1.7 copy.84
  198.9 1.7 copy.86
  200.6 4.1 select_maximum_fusion.2
  204.9 0.7 fusion.36
  205.7 1.1 fusion.72
  206.8 1.9 collective-permute-start.6
  208.7 3.6 collective-permute-start.7
  212.4 7.8 %fusion.7 = f32[3,16,64,128]{3,2,1,0:T(8,128)} fusion(f32[3,16,64,128]{3,2,1,0:T(8,128)} %copy.80, f32[3,16,64,1]{3,2,1,0:T(8,128)} %copy.84, f32[3,16,64,1]{3,2,1,0:T(8,128)} %copy.86, f32[3,18,66,130]{3,2,1,0:T(8,128)S(1)} %select_maximum_fusion.2, f32[16,64,128]{2,1,0:T(8,128)S(1)} %copy-done.11), kind=kLoop, calls=%fused_computation.28 | loop fusion | flops 4325376 | bytes 9986048 | tf_op jit(solution)/shard_map/add | solution.py:85
  220.2 1.7 select_maximum_fusion.8
  221.9 0.6 fusion.31
  222.5 2.1 fusion.34
  224.7 0.8 copy-done.24
  225.4 1.2 multiply_reduce_fusion.2
  226.7 74.8 %psum.52 = f32[]{:T(128)} all-reduce(f32[]{:T(128)} %multiply_reduce_fusion.2), channel_id=1, replica_groups=mesh['len'=16,'xs'=8] {'len','xs'}, use_global_device_ids=true, to_apply=%region_7.8 | all-reduce | flops 1 | bytes 8 | tf_op jit(solution)/shard_map/psum | solution.py:124
  302.8 4.7 multiply_reduce_fusion.1
  307.5 62.8 %psum.53 = f32[]{:T(128)} all-reduce(f32[]{:T(128)} %get-tuple-element.28), channel_id=1, replica_groups=mesh['len'=16,'xs'=8] {'len','xs'}, use_global_device_ids=true, to_apply=%region_9.10 | all-reduce | flops 1 | bytes 8 | tf_op jit(solution)/shard_map/psum | solution.py:128
  371.6 1.7 multiply_add_fusion.1
  373.3 2.2 fusion.68
  375.5 1.9 copy.97
  377.5 2.6 collective-permute-start.9
  380.0 1.9 copy.96
  382.0 3.0 collective-permute-start.8
  385.0 2.8 copy.94
  387.8 1.7 copy.100
  389.4 1.7 copy.98
  391.1 4.3 select_maximum_fusion
  395.7 0.7 fusion.26
  396.5 1.2 fusion.71
  397.7 1.9 collective-permute-start.10
  399.6 3.9 collective-permute-start.11
  403.5 7.7 %fusion.4 = f32[3,16,64,128]{3,2,1,0:T(8,128)} fusion(f32[3,16,64,128]{3,2,1,0:T(8,128)} %copy.94, f32[3,16,64,1]{3,2,1,0:T(8,128)} %copy.98, f32[3,16,64,1]{3,2,1,0:T(8,128)} %copy.100, f32[3,18,66,130]{3,2,1,0:T(8,128)S(1)} %select_maximum_fusion, f32[16,64,128]{2,1,0:T(8,128)S(1)} %copy-done.12), kind=kLoop, calls=%fused_computation.19 | loop fusion | flops 4325376 | bytes 9986048 | tf_op jit(solution)/shard_map/add | solution.py:85
  411.1 1.7 select_maximum_fusion.6
  412.9 0.6 fusion.21
  413.5 2.1 fusion.24
  415.7 1.3 multiply_reduce_fusion
  417.2 71.9 %psum.54 = f32[]{:T(128)} all-reduce(f32[]{:T(128)} %multiply_reduce_fusion), channel_id=1, replica_groups=mesh['len'=16,'xs'=8] {'len','xs'}, use_global_device_ids=true, to_apply=%region_11.12 | all-reduce | flops 1 | bytes 8 | tf_op jit(solution)/shard_map/psum | solution.py:124
  490.4 2.1 multiply_add_fusion
  493.7 1.2 copy.109
  495.2 63.5 %psum.55 = f32[3,256]{1,0:T(4,128)S(1)} all-reduce(f32[3,256]{1,0:T(4,128)S(1)} %fusion.16), channel_id=1, replica_groups=mesh['len'=16,'xs'=8] {'len','xs'}, use_global_device_ids=true, to_apply=%region_14.15 | all-reduce | flops 768 | bytes 6144 | tf_op jit(solution)/shard_map/psum | solution.py:132
  559.7 1.3 copy.110
  (94 shorter events, 6.6 us)
Async XLA Ops:
  3.2 7.6 %copy-start.29 = (s32[2]{0:T(128)S(1)}, s32[2]{0:T(128)}, u32[]{:S(2)}) copy-start(s32[2]{0:T(128)} %constant.71.clone) | copy-start | bytes 28
  3.2 7.8 %copy-start.28 = (s32[128]{0:T(128)S(1)}, s32[128]{0:T(128)}, u32[]{:S(2)}) copy-start(s32[128]{0:T(128)} %param.11) | copy-start | bytes 1540
  3.8 7.5 %collective-permute-start = (f32[3,16,64,1]{2,1,3,0:T(8,128)S(1)}, f32[3,16,64,1]{2,1,3,0:T(8,128)S(1)}, u32[]{:S(2)}, u32[]{:S(2)}) collective-permute-start(f32[3,16,64,1]{2,1,3,0:T(8,128)S(1)} %copy.111), channel_id=1, source_target_pairs={{0,1},{1,2},{2,3},{3,4},{4,5},{5,6},{6,7},{7,8},{8,9},{9,10},{10,1... | collective-permute-start | bytes 36872 | tf_op jit(solution)/shard_map/ppermute | solution.py:24
  8.9 5.2 collective-permute-start.1
  11.3 4.4 copy-start
  11.8 7.7 %copy-start.6 = (f32[3,16,64,1]{3,2,1,0:T(8,128)}, f32[3,16,64,1]{3,2,1,0:T(8,128)S(1)}, u32[]{:S(2)}) copy-start(f32[3,16,64,1]{3,2,1,0:T(8,128)S(1)} %copy.70) | copy-start | bytes 36868
  19.9 6.8 %copy-start.8 = (f32[3,16,64,1]{3,2,1,0:T(8,128)S(1)}, f32[3,16,64,1]{3,2,1,0:T(8,128)}, u32[]{:S(2)}) copy-start(f32[3,16,64,1]{3,2,1,0:T(8,128)} %copy.71) | copy-start | bytes 36868
  20.8 6.0 %copy-start.7 = (f32[3,16,64,1]{3,2,1,0:T(8,128)S(1)}, f32[3,16,64,1]{3,2,1,0:T(8,128)}, u32[]{:S(2)}) copy-start(f32[3,16,64,1]{3,2,1,0:T(8,128)} %copy-done.6) | copy-start | bytes 36868
  20.8 6.0 %copy-start.10 = (f32[16,64,128]{2,1,0:T(8,128)S(1)}, f32[16,64,128]{2,1,0:T(8,128)}, u32[]{:S(2)}) copy-start(f32[16,64,128]{2,1,0:T(8,128)} %param.10) | copy-start | bytes 1572868
  21.0 10.6 %collective-permute-start.2 = (f32[16,64,1]{2,1,0:T(8,128)S(1)}, f32[16,64,1]{2,1,0:T(8,128)S(1)}, u32[]{:S(2)}, u32[]{:S(2)}) collective-permute-start(f32[16,64,1]{2,1,0:T(8,128)S(1)} %get-tuple-element.60), channel_id=1, source_target_pairs={{1,0},{2,1},{3,2},{4,3},{5,4},{6,5},{7,6},{8,7},{9,8},{10,9},{11,1... | collective-permute-start | bytes 12296 | tf_op jit(solution)/shard_map/ppermute | solution.py:26
  23.0 9.8 %collective-permute-start.3 = (f32[16,64,1]{2,1,0:T(8,128)S(1)}, f32[16,64,1]{2,1,0:T(8,128)S(1)}, u32[]{:S(2)}, u32[]{:S(2)}) collective-permute-start(f32[16,64,1]{2,1,0:T(8,128)S(1)} %get-tuple-element.59), channel_id=1, source_target_pairs={{0,1},{1,2},{2,3},{3,4},{4,5},{5,6},{6,7},{7,8},{8,9},{9,10},{10,1... | collective-permute-start | bytes 12296 | tf_op jit(solution)/shard_map/ppermute | solution.py:24
  34.4 1.3 copy-start.19
  34.4 1.3 copy-start.20
  34.4 1.3 copy-start.21
  189.5 7.7 %collective-permute-start.4 = (f32[3,16,64,1]{2,1,3,0:T(8,128)S(1)}, f32[3,16,64,1]{2,1,3,0:T(8,128)S(1)}, u32[]{:S(2)}, u32[]{:S(2)}) collective-permute-start(f32[3,16,64,1]{2,1,3,0:T(8,128)S(1)} %copy.82), channel_id=1, source_target_pairs={{0,1},{1,2},{2,3},{3,4},{4,5},{5,6},{6,7},{7,8},{8,9},{9,10},{10,1... | collective-permute-start | bytes 36872 | tf_op jit(solution)/shard_map/ppermute | solution.py:24
  193.3 5.5 collective-permute-start.5
  205.7 6.7 %copy-start.11 = (f32[16,64,128]{2,1,0:T(8,128)S(1)}, f32[16,64,128]{2,1,0:T(8,128)}, u32[]{:S(2)}) copy-start(f32[16,64,128]{2,1,0:T(8,128)} %param.10) | copy-start | bytes 1572868
  206.8 13.4 %collective-permute-start.6 = (f32[16,64,1]{2,1,0:T(8,128)}, f32[16,64,1]{2,1,0:T(8,128)}, u32[]{:S(2)}, u32[]{:S(2)}) collective-permute-start(f32[16,64,1]{2,1,0:T(8,128)} %get-tuple-element.58), channel_id=1, source_target_pairs={{1,0},{2,1},{3,2},{4,3},{5,4},{6,5},{7,6},{8,7},{9,8},{10,9},{11,1... | collective-permute-start | bytes 12296 | tf_op jit(solution)/shard_map/ppermute | solution.py:26
  208.7 11.4 %collective-permute-start.7 = (f32[16,64,1]{2,1,0:T(8,128)}, f32[16,64,1]{2,1,0:T(8,128)}, u32[]{:S(2)}, u32[]{:S(2)}) collective-permute-start(f32[16,64,1]{2,1,0:T(8,128)} %get-tuple-element.57), channel_id=1, source_target_pairs={{0,1},{1,2},{2,3},{3,4},{4,5},{5,6},{6,7},{7,8},{8,9},{9,10},{10,1... | collective-permute-start | bytes 12296 | tf_op jit(solution)/shard_map/ppermute | solution.py:24
  222.5 2.1 copy-start.22
  222.5 2.1 copy-start.23
  222.5 2.9 copy-start.5
  224.6 0.8 copy-start.24
  373.3 2.2 copy-start.1
  377.5 10.3 %collective-permute-start.9 = (f32[3,16,64,1]{2,1,3,0:T(8,128)S(1)}, f32[3,16,64,1]{2,1,3,0:T(8,128)S(1)}, u32[]{:S(2)}, u32[]{:S(2)}) collective-permute-start(f32[3,16,64,1]{2,1,3,0:T(8,128)S(1)} %copy.97), channel_id=1, source_target_pairs={{1,0},{2,1},{3,2},{4,3},{5,4},{6,5},{7,6},{8,7},{9,8},{10,9},{11,1... | collective-permute-start | bytes 36872 | tf_op jit(solution)/shard_map/ppermute | solution.py:26
  382.0 7.5 %collective-permute-start.8 = (f32[3,16,64,1]{2,1,3,0:T(8,128)S(1)}, f32[3,16,64,1]{2,1,3,0:T(8,128)S(1)}, u32[]{:S(2)}, u32[]{:S(2)}) collective-permute-start(f32[3,16,64,1]{2,1,3,0:T(8,128)S(1)} %copy.96), channel_id=1, source_target_pairs={{0,1},{1,2},{2,3},{3,4},{4,5},{5,6},{6,7},{7,8},{8,9},{9,10},{10,1... | collective-permute-start | bytes 36872 | tf_op jit(solution)/shard_map/ppermute | solution.py:24
  396.5 7.0 %copy-start.12 = (f32[16,64,128]{2,1,0:T(8,128)S(1)}, f32[16,64,128]{2,1,0:T(8,128)}, u32[]{:S(2)}) copy-start(f32[16,64,128]{2,1,0:T(8,128)} %param.10) | copy-start | bytes 1572868
  397.7 13.4 %collective-permute-start.10 = (f32[16,64,1]{2,1,0:T(8,128)}, f32[16,64,1]{2,1,0:T(8,128)}, u32[]{:S(2)}, u32[]{:S(2)}) collective-permute-start(f32[16,64,1]{2,1,0:T(8,128)} %get-tuple-element.56), channel_id=1, source_target_pairs={{1,0},{2,1},{3,2},{4,3},{5,4},{6,5},{7,6},{8,7},{9,8},{10,9},{11,1... | collective-permute-start | bytes 12296 | tf_op jit(solution)/shard_map/ppermute | solution.py:26
  399.6 11.5 %collective-permute-start.11 = (f32[16,64,1]{2,1,0:T(8,128)}, f32[16,64,1]{2,1,0:T(8,128)}, u32[]{:S(2)}, u32[]{:S(2)}) collective-permute-start(f32[16,64,1]{2,1,0:T(8,128)} %get-tuple-element.55), channel_id=1, source_target_pairs={{0,1},{1,2},{2,3},{3,4},{4,5},{5,6},{6,7},{7,8},{8,9},{9,10},{10,1... | collective-permute-start | bytes 12296 | tf_op jit(solution)/shard_map/ppermute | solution.py:24
  412.8 2.8 copy-start.3
  413.5 3.5 copy-start.13
  413.5 3.5 copy-start.15
  413.5 2.2 copy-start.2
  415.6 1.4 copy-start.17
  490.3 2.1 copy-start.4
  490.3 2.3 copy-start.9
  490.4 2.4 copy-start.14
  490.4 2.6 copy-start.16
  490.4 2.7 copy-start.18
  493.6 65.1 %copy-start.25 = (f32[2,256]{1,0:T(2,128)S(1)}, f32[2,256]{1,0:T(2,128)}, u32[]{:S(2)}) copy-start(f32[2,256]{1,0:T(2,128)} %param.14) | copy-start | bytes 6148
  493.6 65.1 %copy-start.26 = (f32[256]{0:T(256)S(1)}, f32[256]{0:T(256)}, u32[]{:S(2)}) copy-start(f32[256]{0:T(256)} %param.13) | copy-start | bytes 3076
  493.7 65.1 %copy-start.27 = (s32[256]{0:T(256)S(1)}, s32[256]{0:T(256)}, u32[]{:S(2)}) copy-start(s32[256]{0:T(256)} %param.12) | copy-start | bytes 3076
where the time goes:
time: 570 us; the launch traced here: 561 us
  blocking collectives  414 us (73%)
  other arithmetic  63.3 us (11%)
  local copies, waits for them, and re-layouts  36.9 us (6%)
  starting transfers between devices  33.4 us (6%)
  between operations  8.1 us (1%)
    psum x2, blocking collectives, shards(): curvature = lax.psum(jnp.sum(direction * image), ('len', 'xs'))  147 us
    psum x2, blocking collectives, shards(): norm_next = lax.psum(jnp.sum(solved * solved), ('len', 'xs'))  128 us
    psum x1, blocking collectives, shards(): norm_now = lax.psum(jnp.sum(solved * solved), ('len', 'xs'))  76.7 us
    psum x1, blocking collectives, shards(): lax.psum(jnp.sum(picked * across_hit[None], axis=1), ('len', 'xs'))  63.5 us
    ppermute x6, starting transfers between devices, extended_2(): lax.ppermute(tail, axis, [(i, (i + 1) % count) for i in range(ends)])  20.7 us
    concatenate x6, other arithmetic, extended_2(): jnp.concatenate([lax.ppermute(tail, axis, [(i, (i + 1) % count) for i in...  16.2 us
    add x2, other arithmetic, operate(): mass_field[None] * field + shear_modulus * laplacian  15.4 us
    slice x8, local copies, waits for them, and re-layouts, extended_2(): lax.slice_in_dim(cells, cells.shape[dim] - width, cells.shape[dim], axis=...  13.4 us
  transfers between devices with their start and end apart: 12, of which 3 were waited for; matrix products, arithmetic and copies ran while one was open for 6% of the time, Pallas kernels for 0%

commit v1 on v0

--- a/solution.py
+++ b/solution.py
@@ -2,6 +2,7 @@
 import jax.numpy as jnp
 from jax import lax
 from jax.sharding import PartitionSpec as P
+from jax.lax import all_gather
 
 ITERS = 3
 shear_modulus = 1.0
@@ -129,7 +130,8 @@
         direction = solved + norm_next / norm_now * direction
         norm_now = norm_next
     picked = jnp.einsum("csl,lb->csb", increment[:, 0], along_hit, precision=lax.Precision.HIGHEST)
-    readout = lax.psum(jnp.sum(picked * across_hit[None], axis=1), ("len", "xs"))
+    z = jnp.sum(picked * across_hit[None], axis=1)
+    readout = jnp.sum(all_gather(z, axis_name=("len", "xs")), axis=0)
     friction, force = return_map(readout, stick_flags, normal_load, prior_friction)
     spread = force[:, None, :] * across_hit[None]
     placed = jnp.einsum("csb,lb->csl", spread, along_hit, precision=lax.Precision.HIGHEST)

time: 570 us -> 541 us (0.949)
  blocking collectives: 414 us -> 386 us
    psum x1 -> x0, blocking collectives: 63.5 us -> none  [shards(): lax.psum(jnp.sum(picked * across_hit[None], axis=1), ('len', 'xs'))]
    all_gather x0 -> x1, blocking collectives: none -> 34.5 us  [shards(): readout = jnp.sum(all_gather(z, axis_name=('len', 'xs')), axis=0)]
where the time goes in v1:
time: 541 us; the launch traced here: 532 us
  blocking collectives  386 us (71%)
  other arithmetic  63.5 us (12%)
  local copies, waits for them, and re-layouts  36.9 us (7%)
  starting transfers between devices  33.4 us (6%)
  between operations  8.11 us (1%)
    psum x2, blocking collectives, shards(): curvature = lax.psum(jnp.sum(direction * image), ('len', 'xs'))  147 us
    psum x2, blocking collectives, shards(): norm_next = lax.psum(jnp.sum(solved * solved), ('len', 'xs'))  128 us
    psum x1, blocking collectives, shards(): norm_now = lax.psum(jnp.sum(solved * solved), ('len', 'xs'))  76.7 us
    all_gather x1, blocking collectives, shards(): readout = jnp.sum(all_gather(z, axis_name=('len', 'xs')), axis=0)  34.5 us
    ppermute x6, starting transfers between devices, extended_2(): lax.ppermute(tail, axis, [(i, (i + 1) % count) for i in range(ends)])  20.7 us
    concatenate x6, other arithmetic, extended_2(): jnp.concatenate([lax.ppermute(tail, axis, [(i, (i + 1) % count) for i in...  16.2 us
    add x2, other arithmetic, operate(): mass_field[None] * field + shear_modulus * laplacian  15.4 us
    slice x8, local copies, waits for them, and re-layouts, extended_2(): lax.slice_in_dim(cells, cells.shape[dim] - width, cells.shape[dim], axis=...  13.4 us
  transfers between devices with their start and end apart: 12, of which 3 were waited for; matrix products, arithmetic and copies ran while one was open for 6% of the time, Pallas kernels for 0%

profile of v1, /device:TPU:1, one launch (start us, length us, event | category | flops | bytes accessed | tf_op | source)
XLA Modules:
  0.0 532.5 jit_solution(12798461597493720446)
XLA Ops:
  0.6 2.6 fusion.70
  3.8 4.6 collective-permute-start
  8.9 1.9 collective-permute-start.1
  11.8 2.2 collective-permute-done.1
  14.0 1.7 copy.71
  15.7 3.8 select_maximum_fusion.4
  19.9 0.8 fusion.46
  21.0 2.0 collective-permute-start.2
  23.0 3.6 collective-permute-start.3
  26.7 3.9 multiply_reduce_fusion.5
  30.6 1.0 collective-permute-done.2
  31.6 1.2 collective-permute-done.3
  33.3 1.0 fusion.41
  34.4 1.3 multiply_reduce_fusion.4
  35.7 76.7 %all-reduce.6 = (f32[]{:T(128)}, f32[]{:T(128)}) all-reduce(f32[]{:T(128)} %get-tuple-element.45, f32[]{:T(128)} %multiply_reduce_fusion.4), channel_id=1, replica_groups=mesh['len'=16,'xs'=8] {'len','xs'}, use_global_device_ids=true, to_apply=%region_1.2 | all-reduce | flops 2 | bytes 16 | tf_op jit(solution)/shard_map/psum | solution.py:122
  113.7 3.6 multiply_reduce_fusion.3
  117.3 64.9 %psum.44 = f32[]{:T(128)} all-reduce(f32[]{:T(128)} %get-tuple-element.30), channel_id=1, replica_groups=mesh['len'=16,'xs'=8] {'len','xs'}, use_global_device_ids=true, to_apply=%region_5.6 | all-reduce | flops 1 | bytes 8 | tf_op jit(solution)/shard_map/psum | solution.py:129
  183.5 1.8 multiply_add_fusion.2
  185.3 2.3 fusion.69
  187.6 1.9 copy.82
  189.5 1.9 collective-permute-start.4
  191.4 1.9 copy.83
  193.3 2.4 collective-permute-start.5
  195.9 1.3 copy.80
  197.2 1.7 copy.84
  198.9 1.7 copy.86
  200.6 4.1 select_maximum_fusion.2
  204.9 0.7 fusion.36
  205.7 1.1 fusion.72
  206.8 1.9 collective-permute-start.6
  208.7 3.6 collective-permute-start.7
  212.4 7.8 %fusion.7 = f32[3,16,64,128]{3,2,1,0:T(8,128)} fusion(f32[3,16,64,128]{3,2,1,0:T(8,128)} %copy.80, f32[3,16,64,1]{3,2,1,0:T(8,128)} %copy.84, f32[3,16,64,1]{3,2,1,0:T(8,128)} %copy.86, f32[3,18,66,130]{3,2,1,0:T(8,128)S(1)} %select_maximum_fusion.2, f32[16,64,128]{2,1,0:T(8,128)S(1)} %copy-done.11), kind=kLoop, calls=%fused_computation.28 | loop fusion | flops 4325376 | bytes 9986048 | tf_op jit(solution)/shard_map/add | solution.py:86
  220.2 1.7 select_maximum_fusion.8
  221.9 0.6 fusion.31
  222.5 2.1 fusion.34
  224.7 0.8 copy-done.24
  225.4 1.2 multiply_reduce_fusion.2
  226.7 74.8 %psum.45 = f32[]{:T(128)} all-reduce(f32[]{:T(128)} %multiply_reduce_fusion.2), channel_id=1, replica_groups=mesh['len'=16,'xs'=8] {'len','xs'}, use_global_device_ids=true, to_apply=%region_7.8 | all-reduce | flops 1 | bytes 8 | tf_op jit(solution)/shard_map/psum | solution.py:125
  302.8 4.7 multiply_reduce_fusion.1
  307.5 62.8 %psum.46 = f32[]{:T(128)} all-reduce(f32[]{:T(128)} %get-tuple-element.28), channel_id=1, replica_groups=mesh['len'=16,'xs'=8] {'len','xs'}, use_global_device_ids=true, to_apply=%region_9.10 | all-reduce | flops 1 | bytes 8 | tf_op jit(solution)/shard_map/psum | solution.py:129
  371.6 1.7 multiply_add_fusion.1
  373.3 2.2 fusion.68
  375.5 1.9 copy.97
  377.5 2.6 collective-permute-start.9
  380.0 1.9 copy.96
  382.0 3.0 collective-permute-start.8
  385.0 2.8 copy.94
  387.8 1.7 copy.100
  389.4 1.7 copy.98
  391.1 4.3 select_maximum_fusion
  395.7 0.7 fusion.26
  396.5 1.2 fusion.71
  397.7 1.9 collective-permute-start.10
  399.6 3.9 collective-permute-start.11
  403.5 7.7 %fusion.4 = f32[3,16,64,128]{3,2,1,0:T(8,128)} fusion(f32[3,16,64,128]{3,2,1,0:T(8,128)} %copy.94, f32[3,16,64,1]{3,2,1,0:T(8,128)} %copy.98, f32[3,16,64,1]{3,2,1,0:T(8,128)} %copy.100, f32[3,18,66,130]{3,2,1,0:T(8,128)S(1)} %select_maximum_fusion, f32[16,64,128]{2,1,0:T(8,128)S(1)} %copy-done.12), kind=kLoop, calls=%fused_computation.19 | loop fusion | flops 4325376 | bytes 9986048 | tf_op jit(solution)/shard_map/add | solution.py:86
  411.1 1.7 select_maximum_fusion.6
  412.9 0.6 fusion.21
  413.5 2.1 fusion.24
  415.7 1.3 multiply_reduce_fusion
  417.2 71.9 %psum.47 = f32[]{:T(128)} all-reduce(f32[]{:T(128)} %multiply_reduce_fusion), channel_id=1, replica_groups=mesh['len'=16,'xs'=8] {'len','xs'}, use_global_device_ids=true, to_apply=%region_11.12 | all-reduce | flops 1 | bytes 8 | tf_op jit(solution)/shard_map/psum | solution.py:125
  490.4 2.1 multiply_add_fusion
  493.7 1.2 copy.109
  495.2 34.5 %all-gather.1 = f32[128,3,256]{2,1,0:T(4,128)S(1)} all-gather(f32[1,3,256]{2,1,0:T(4,128)S(1)} %bitcast.57), channel_id=2, replica_groups=mesh['len'=16,'xs'=8] {'len','xs'}, dimensions={0}, use_global_device_ids=true | all-gather | bytes 396288 | tf_op jit(solution)/shard_map/all_gather | solution.py:134
  530.9 1.3 copy.110
  (95 shorter events, 6.7 us)
Async XLA Ops:
  3.2 7.6 %copy-start.29 = (s32[2]{0:T(128)S(1)}, s32[2]{0:T(128)}, u32[]{:S(2)}) copy-start(s32[2]{0:T(128)} %constant.71.clone) | copy-start | bytes 28
  3.2 7.8 %copy-start.28 = (s32[128]{0:T(128)S(1)}, s32[128]{0:T(128)}, u32[]{:S(2)}) copy-start(s32[128]{0:T(128)} %param.11) | copy-start | bytes 1540
  3.8 7.5 %collective-permute-start = (f32[3,16,64,1]{2,1,3,0:T(8,128)S(1)}, f32[3,16,64,1]{2,1,3,0:T(8,128)S(1)}, u32[]{:S(2)}, u32[]{:S(2)}) collective-permute-start(f32[3,16,64,1]{2,1,3,0:T(8,128)S(1)} %copy.111), channel_id=1, source_target_pairs={{0,1},{1,2},{2,3},{3,4},{4,5},{5,6},{6,7},{7,8},{8,9},{9,10},{10,1... | collective-permute-start | bytes 36872 | tf_op jit(solution)/shard_map/ppermute | solution.py:25
  8.9 5.2 collective-permute-start.1
  11.3 4.4 copy-start
  11.8 7.7 %copy-start.6 = (f32[3,16,64,1]{3,2,1,0:T(8,128)}, f32[3,16,64,1]{3,2,1,0:T(8,128)S(1)}, u32[]{:S(2)}) copy-start(f32[3,16,64,1]{3,2,1,0:T(8,128)S(1)} %copy.70) | copy-start | bytes 36868
  19.9 6.8 %copy-start.8 = (f32[3,16,64,1]{3,2,1,0:T(8,128)S(1)}, f32[3,16,64,1]{3,2,1,0:T(8,128)}, u32[]{:S(2)}) copy-start(f32[3,16,64,1]{3,2,1,0:T(8,128)} %copy.71) | copy-start | bytes 36868
  20.8 6.0 %copy-start.7 = (f32[3,16,64,1]{3,2,1,0:T(8,128)S(1)}, f32[3,16,64,1]{3,2,1,0:T(8,128)}, u32[]{:S(2)}) copy-start(f32[3,16,64,1]{3,2,1,0:T(8,128)} %copy-done.6) | copy-start | bytes 36868
  20.8 6.0 %copy-start.10 = (f32[16,64,128]{2,1,0:T(8,128)S(1)}, f32[16,64,128]{2,1,0:T(8,128)}, u32[]{:S(2)}) copy-start(f32[16,64,128]{2,1,0:T(8,128)} %param.10) | copy-start | bytes 1572868
  21.0 10.6 %collective-permute-start.2 = (f32[16,64,1]{2,1,0:T(8,128)S(1)}, f32[16,64,1]{2,1,0:T(8,128)S(1)}, u32[]{:S(2)}, u32[]{:S(2)}) collective-permute-start(f32[16,64,1]{2,1,0:T(8,128)S(1)} %get-tuple-element.60), channel_id=1, source_target_pairs={{1,0},{2,1},{3,2},{4,3},{5,4},{6,5},{7,6},{8,7},{9,8},{10,9},{11,1... | collective-permute-start | bytes 12296 | tf_op jit(solution)/shard_map/ppermute | solution.py:27
  23.0 9.8 %collective-permute-start.3 = (f32[16,64,1]{2,1,0:T(8,128)S(1)}, f32[16,64,1]{2,1,0:T(8,128)S(1)}, u32[]{:S(2)}, u32[]{:S(2)}) collective-permute-start(f32[16,64,1]{2,1,0:T(8,128)S(1)} %get-tuple-element.59), channel_id=1, source_target_pairs={{0,1},{1,2},{2,3},{3,4},{4,5},{5,6},{6,7},{7,8},{8,9},{9,10},{10,1... | collective-permute-start | bytes 12296 | tf_op jit(solution)/shard_map/ppermute | solution.py:25
  34.4 1.3 copy-start.19
  34.4 1.3 copy-start.20
  34.4 1.3 copy-start.21
  189.5 7.7 %collective-permute-start.4 = (f32[3,16,64,1]{2,1,3,0:T(8,128)S(1)}, f32[3,16,64,1]{2,1,3,0:T(8,128)S(1)}, u32[]{:S(2)}, u32[]{:S(2)}) collective-permute-start(f32[3,16,64,1]{2,1,3,0:T(8,128)S(1)} %copy.82), channel_id=1, source_target_pairs={{0,1},{1,2},{2,3},{3,4},{4,5},{5,6},{6,7},{7,8},{8,9},{9,10},{10,1... | collective-permute-start | bytes 36872 | tf_op jit(solution)/shard_map/ppermute | solution.py:25
  193.3 5.5 %collective-permute-start.5 = (f32[3,16,64,1]{2,1,3,0:T(8,128)S(1)}, f32[3,16,64,1]{2,1,3,0:T(8,128)S(1)}, u32[]{:S(2)}, u32[]{:S(2)}) collective-permute-start(f32[3,16,64,1]{2,1,3,0:T(8,128)S(1)} %copy.83), channel_id=1, source_target_pairs={{1,0},{2,1},{3,2},{4,3},{5,4},{6,5},{7,6},{8,7},{9,8},{10,9},{11,1... | collective-permute-start | bytes 36872 | tf_op jit(solution)/shard_map/ppermute | solution.py:27
  205.7 6.7 %copy-start.11 = (f32[16,64,128]{2,1,0:T(8,128)S(1)}, f32[16,64,128]{2,1,0:T(8,128)}, u32[]{:S(2)}) copy-start(f32[16,64,128]{2,1,0:T(8,128)} %param.10) | copy-start | bytes 1572868
  206.8 13.4 %collective-permute-start.6 = (f32[16,64,1]{2,1,0:T(8,128)}, f32[16,64,1]{2,1,0:T(8,128)}, u32[]{:S(2)}, u32[]{:S(2)}) collective-permute-start(f32[16,64,1]{2,1,0:T(8,128)} %get-tuple-element.58), channel_id=1, source_target_pairs={{1,0},{2,1},{3,2},{4,3},{5,4},{6,5},{7,6},{8,7},{9,8},{10,9},{11,1... | collective-permute-start | bytes 12296 | tf_op jit(solution)/shard_map/ppermute | solution.py:27
  208.7 11.4 %collective-permute-start.7 = (f32[16,64,1]{2,1,0:T(8,128)}, f32[16,64,1]{2,1,0:T(8,128)}, u32[]{:S(2)}, u32[]{:S(2)}) collective-permute-start(f32[16,64,1]{2,1,0:T(8,128)} %get-tuple-element.57), channel_id=1, source_target_pairs={{0,1},{1,2},{2,3},{3,4},{4,5},{5,6},{6,7},{7,8},{8,9},{9,10},{10,1... | collective-permute-start | bytes 12296 | tf_op jit(solution)/shard_map/ppermute | solution.py:25
  222.5 2.1 copy-start.22
  222.5 2.1 copy-start.23
  222.5 2.9 copy-start.5
  224.6 0.8 copy-start.24
  373.3 2.2 copy-start.1
  377.5 10.3 %collective-permute-start.9 = (f32[3,16,64,1]{2,1,3,0:T(8,128)S(1)}, f32[3,16,64,1]{2,1,3,0:T(8,128)S(1)}, u32[]{:S(2)}, u32[]{:S(2)}) collective-permute-start(f32[3,16,64,1]{2,1,3,0:T(8,128)S(1)} %copy.97), channel_id=1, source_target_pairs={{1,0},{2,1},{3,2},{4,3},{5,4},{6,5},{7,6},{8,7},{9,8},{10,9},{11,1... | collective-permute-start | bytes 36872 | tf_op jit(solution)/shard_map/ppermute | solution.py:27
  382.0 7.5 %collective-permute-start.8 = (f32[3,16,64,1]{2,1,3,0:T(8,128)S(1)}, f32[3,16,64,1]{2,1,3,0:T(8,128)S(1)}, u32[]{:S(2)}, u32[]{:S(2)}) collective-permute-start(f32[3,16,64,1]{2,1,3,0:T(8,128)S(1)} %copy.96), channel_id=1, source_target_pairs={{0,1},{1,2},{2,3},{3,4},{4,5},{5,6},{6,7},{7,8},{8,9},{9,10},{10,1... | collective-permute-start | bytes 36872 | tf_op jit(solution)/shard_map/ppermute | solution.py:25
  396.5 7.0 %copy-start.12 = (f32[16,64,128]{2,1,0:T(8,128)S(1)}, f32[16,64,128]{2,1,0:T(8,128)}, u32[]{:S(2)}) copy-start(f32[16,64,128]{2,1,0:T(8,128)} %param.10) | copy-start | bytes 1572868
  397.7 13.4 %collective-permute-start.10 = (f32[16,64,1]{2,1,0:T(8,128)}, f32[16,64,1]{2,1,0:T(8,128)}, u32[]{:S(2)}, u32[]{:S(2)}) collective-permute-start(f32[16,64,1]{2,1,0:T(8,128)} %get-tuple-element.56), channel_id=1, source_target_pairs={{1,0},{2,1},{3,2},{4,3},{5,4},{6,5},{7,6},{8,7},{9,8},{10,9},{11,1... | collective-permute-start | bytes 12296 | tf_op jit(solution)/shard_map/ppermute | solution.py:27
  399.6 11.5 %collective-permute-start.11 = (f32[16,64,1]{2,1,0:T(8,128)}, f32[16,64,1]{2,1,0:T(8,128)}, u32[]{:S(2)}, u32[]{:S(2)}) collective-permute-start(f32[16,64,1]{2,1,0:T(8,128)} %get-tuple-element.55), channel_id=1, source_target_pairs={{0,1},{1,2},{2,3},{3,4},{4,5},{5,6},{6,7},{7,8},{8,9},{9,10},{10,1... | collective-permute-start | bytes 12296 | tf_op jit(solution)/shard_map/ppermute | solution.py:25
  412.8 2.8 copy-start.3
  413.5 3.5 copy-start.13
  413.5 3.5 copy-start.15
  413.5 2.2 copy-start.2
  415.6 1.4 copy-start.17
  490.3 2.1 copy-start.4
  490.3 2.3 copy-start.9
  490.4 2.4 copy-start.14
  490.4 2.6 copy-start.16
  490.4 2.7 copy-start.18
  493.6 36.3 %copy-start.25 = (f32[2,256]{1,0:T(2,128)S(1)}, f32[2,256]{1,0:T(2,128)}, u32[]{:S(2)}) copy-start(f32[2,256]{1,0:T(2,128)} %param.14) | copy-start | bytes 6148
  493.6 36.3 %copy-start.26 = (f32[256]{0:T(256)S(1)}, f32[256]{0:T(256)}, u32[]{:S(2)}) copy-start(f32[256]{0:T(256)} %param.13) | copy-start | bytes 3076
  493.7 36.3 %copy-start.27 = (s32[256]{0:T(256)S(1)}, s32[256]{0:T(256)}, u32[]{:S(2)}) copy-start(s32[256]{0:T(256)} %param.12) | copy-start | bytes 3076
